TPU v7x, 32 devices: a whole 2x2x4 slice. The times are simulated.
32 devices in a mesh: groups: 2 (over x), tok: 16 (over z, y, core).
Axes of the slice: x: 2, y: 2, z: 4, core: 2. Of those that a mesh axis runs over, the one named last changes fastest.
Arguments:
- query_tokens: bfloat16 [3, 4096, 1024], P(None, ('groups', 'tok')), parts along dimension 1, may hold values from -6 to 6
- key_tokens: bfloat16 [3, 4096, 1024], P(None, ('groups', 'tok')), parts along dimension 1, may hold values from -6 to 6
- value_tokens: bfloat16 [3, 4096, 1024], P(None, ('groups', 'tok')), parts along dimension 1, may hold values from -6 to 6
- learn_rates: float32 [3, 4096, 2], P(None, ('groups', 'tok')), parts along dimension 1, may hold values from 0.0009765625 to 0.00390625
- fast_first: bfloat16 [2, 512, 512], P(None, 'tok'), may hold values from -0.25 to 0.25
- fast_third: bfloat16 [2, 512, 512], P(None, 'tok'), may hold values from -0.25 to 0.25
- fast_second: bfloat16 [2, 512, 512], P(None, 'tok'), may hold values from -0.25 to 0.25
- momentum_decay: float32 [2], replicated, may hold values from 0.3 to 0.95
Outputs:
- readout: bfloat16 [3, 4096, 1024], P(None, ('groups', 'tok')), parts along dimension 1
There are 2 independent parts, one for each index of `groups`. A program takes and returns all parts, laid end to end along the dimension named above; an argument that names none is the same for every part. Nothing has to cross between parts.
All inputs are finite; a program needn't handle non-finite values.
Results may differ from a plain program's by a relative error of at most 0.0089.
Values may be sent and summed in bfloat16 or wider, within the bound.
A program may use at most 64 MiB of HBM per device.

v0:
```python
import jax
import jax.numpy as jnp
from jax import lax
from jax.sharding import PartitionSpec as P


def forward_parts(weights, inputs):
    first, third, second = weights
    length = inputs.shape[0]
    head_count = first.shape[0]
    shaped = inputs.reshape(length, head_count, -1)
    pre_gate = jnp.einsum("thd,hfd->htf", shaped, first, preferred_element_type=jnp.float32)
    pre_up = jnp.einsum("thd,hfd->htf", shaped, third, preferred_element_type=jnp.float32)
    hidden = (jax.nn.silu(pre_gate) * pre_up).astype(jnp.bfloat16)
    return (shaped, pre_gate, pre_up, hidden)


def apply_block(weights, inputs):
    shaped, pre_gate, pre_up, hidden = forward_parts(weights, inputs)
    result = jnp.einsum("htf,hdf->thd", hidden, weights[2], preferred_element_type=jnp.float32)
    return result.reshape(inputs.shape[0], -1).astype(jnp.bfloat16)


def partial_steps(weights, keys, values, rates):
    shaped, pre_gate, pre_up, hidden = forward_parts(weights, keys)
    length = keys.shape[0]
    head_count = weights[0].shape[0]
    scaled = (
        rates[:, :, None] * values.reshape(length, head_count, -1).astype(jnp.float32)
    ).astype(jnp.bfloat16)
    step_second = jnp.einsum("thd,htf->hdf", scaled, hidden, preferred_element_type=jnp.float32)
    back = jnp.einsum("thd,hdf->htf", scaled, weights[2], preferred_element_type=jnp.float32)
    sig_gate = jax.nn.sigmoid(pre_gate)
    d_gate = (back * pre_up * sig_gate * (1.0 + pre_gate * (1.0 - sig_gate))).astype(jnp.bfloat16)
    d_up = (back * pre_gate * sig_gate).astype(jnp.bfloat16)
    step_first = jnp.einsum("htf,thd->hfd", d_gate, shaped, preferred_element_type=jnp.float32)
    step_third = jnp.einsum("htf,thd->hfd", d_up, shaped, preferred_element_type=jnp.float32)
    return (step_first, step_third, step_second)


def summed_steps(terms):
    return (
        lax.psum_scatter(terms[0], "tok", scatter_dimension=1, tiled=True),
        lax.psum_scatter(terms[1], "tok", scatter_dimension=1, tiled=True),
        lax.psum_scatter(terms[2], "tok", scatter_dimension=1, tiled=True),
    )


def renorm(old, moved):
    old_norm = jnp.sqrt(jnp.sum(old * old, axis=-1, keepdims=True) + 1e-06)
    moved_norm = jnp.sqrt(jnp.sum(moved * moved, axis=-1, keepdims=True) + 1e-06)
    return moved * old_norm / moved_norm


def full_steps(owned):
    return (
        lax.all_gather(owned[0], "tok", axis=1, tiled=True),
        lax.all_gather(owned[1], "tok", axis=1, tiled=True),
        lax.all_gather(owned[2], "tok", axis=1, tiled=True),
    )


def shards(
    query_tokens,
    key_tokens,
    value_tokens,
    learn_rates,
    fast_first,
    fast_third,
    fast_second,
    momentum_decay,
):
    full_zero = (
        lax.all_gather(fast_first, "tok", axis=1, tiled=True),
        lax.all_gather(fast_third, "tok", axis=1, tiled=True),
        lax.all_gather(fast_second, "tok", axis=1, tiled=True),
    )
    out_zero = apply_block(full_zero, query_tokens[0])
    terms_zero = partial_steps(full_zero, key_tokens[0], value_tokens[0], learn_rates[0])
    terms_one = partial_steps(full_zero, key_tokens[1], value_tokens[1], learn_rates[1])
    step_zero = summed_steps(terms_zero)
    decay = momentum_decay[:, None, None]
    weights_zero = tuple((w.astype(jnp.float32) for w in full_zero))
    whole_zero = full_steps(step_zero)
    weights_one = tuple((renorm(w, w + m) for w, m in zip(weights_zero, whole_zero)))
    full_one = tuple((w.astype(jnp.bfloat16) for w in weights_one))
    out_one = apply_block(full_one, query_tokens[1])
    step_one = summed_steps(terms_one)
    whole_one = full_steps(step_one)
    moment = tuple((decay * m + s for m, s in zip(whole_zero, whole_one)))
    weights_two = tuple((renorm(w, w + m) for w, m in zip(weights_one, moment)))
    full_two = tuple((w.astype(jnp.bfloat16) for w in weights_two))
    out_two = apply_block(full_two, query_tokens[2])
    return jnp.stack([out_zero, out_one, out_two])


def solution(mesh):
    placed = (
        P(None, ("groups", "tok"), None),
        P(None, ("groups", "tok"), None),
        P(None, ("groups", "tok"), None),
        P(None, ("groups", "tok"), None),
        P(None, "tok", None),
        P(None, "tok", None),
        P(None, "tok", None),
        P(),
    )
    return jax.shard_map(
        shards,
        mesh=mesh,
        in_specs=placed,
        out_specs=P(None, ("groups", "tok"), None),
        check_vma=False,
    )
```

profile of v0, /device:TPU:0, one launch (start us, length us, event | category | flops | bytes accessed | tf_op | source)
XLA Modules:
  0.0 798.2 jit_solution(18446105568856472642)
XLA Ops:
  6.5 0.7 all-gather.10.cloned.1.call-update
  7.3 0.7 all-gather.12.cloned.1.call-update
  8.1 0.7 all-gather.14.cloned.1.call-update
  8.8 0.0 reduce-scatter.7.cloned.1.call-start
  8.8 1.1 fusion.64
  9.9 0.2 copy.69
  10.1 0.1 slice_convert_fusion.1
  10.2 0.4 reshape.115
  10.6 39.5 %all-gather.10.cloned.1.call-done = bf16[2,512,512]{2,1,0:T(8,128)(2,1)} async-done(((bf16[2,32,512]{2,1,0:T(8,128)(2,1)}), bf16[2,512,512]{2,1,0:T(8,128)(2,1)}) %all-gather.10.cloned.1.call-update) | async-done | bytes 1048592 | tf_op jit(solution)/shard_map/all_gather | solution.py:74
  50.1 1.7 fusion.66
  51.8 37.3 %all-gather.12.cloned.1.call-done = bf16[2,512,512]{2,1,0:T(8,128)(2,1)} async-done(((bf16[2,32,512]{2,1,0:T(8,128)(2,1)}), bf16[2,512,512]{2,1,0:T(8,128)(2,1)}) %all-gather.12.cloned.1.call-update) | async-done | bytes 1048592 | tf_op jit(solution)/shard_map/all_gather | solution.py:75
  89.2 1.7 fusion.67
  90.9 1.9 fusion.33
  92.8 0.0 reduce-scatter.9.cloned.1.call-start
  92.8 35.4 %all-gather.14.cloned.1.call-done = bf16[2,512,512]{2,1,0:T(8,128)(2,1)} async-done(((bf16[2,32,512]{2,1,0:T(8,128)(2,1)}), bf16[2,512,512]{2,1,0:T(8,128)(2,1)}) %all-gather.14.cloned.1.call-update) | async-done | bytes 1048592 | tf_op jit(solution)/shard_map/all_gather | solution.py:76
  128.2 1.6 fusion.48
  129.8 1.9 fusion.34
  131.7 0.0 reduce-scatter.11.cloned.1.call-start
  131.8 1.8 fusion.35
  133.6 0.0 reduce-scatter.13.cloned.1.call-start
  133.7 0.2 copy.71
  133.9 1.2 reshape.116
  135.1 0.5 fusion.68
  135.6 0.5 fusion.69
  136.1 0.3 copy-done.3
  136.4 0.5 copy-done.5
  136.9 1.9 fusion.36
  138.8 0.0 reduce-scatter.15.cloned.1.call-start
  138.9 1.5 fusion.51
  140.4 0.8 copy-done.7
  141.2 1.9 fusion.37
  143.1 0.0 reduce-scatter.17.cloned.1.call-start
  143.2 3.1 fusion.38
  146.2 0.0 all-gather.16.cloned.1.call-start
  146.3 46.3 %reduce-scatter.7.cloned.1.call-done = f32[2,32,512]{2,1,0:T(8,128)} async-done(((f32[2,512,512]{2,1,0:T(8,128)}), f32[2,32,512]{2,1,0:T(8,128)}) %reduce-scatter.7.cloned.1.call-update) | async-done | bytes 131088 | tf_op jit(solution)/shard_map/reduce_scatter | solution.py:45
  192.7 64.3 %reduce-scatter.9.cloned.1.call-done = f32[2,32,512]{2,1,0:T(8,128)} async-done(((f32[2,512,512]{2,1,0:T(8,128)}), f32[2,32,512]{2,1,0:T(8,128)}) %reduce-scatter.9.cloned.1.call-update) | async-done | bytes 131088 | tf_op jit(solution)/shard_map/reduce_scatter | solution.py:43
  257.1 64.3 %reduce-scatter.11.cloned.1.call-done = f32[2,32,512]{2,1,0:T(8,128)} async-done(((f32[2,512,512]{2,1,0:T(8,128)}), f32[2,32,512]{2,1,0:T(8,128)}) %reduce-scatter.11.cloned.1.call-update) | async-done | bytes 131088 | tf_op jit(solution)/shard_map/reduce_scatter | solution.py:44
  321.4 64.5 %reduce-scatter.13.cloned.1.call-done = f32[2,32,512]{2,1,0:T(8,128)} async-done(((f32[2,512,512]{2,1,0:T(8,128)}), f32[2,32,512]{2,1,0:T(8,128)}) %reduce-scatter.13.cloned.1.call-update) | async-done | bytes 131088 | tf_op jit(solution)/shard_map/reduce_scatter | solution.py:45
  386.0 64.4 %reduce-scatter.15.cloned.1.call-done = f32[2,32,512]{2,1,0:T(8,128)} async-done(((f32[2,512,512]{2,1,0:T(8,128)}), f32[2,32,512]{2,1,0:T(8,128)}) %reduce-scatter.15.cloned.1.call-update) | async-done | bytes 131088 | tf_op jit(solution)/shard_map/reduce_scatter | solution.py:43
  450.4 0.2 all-gather.26.cloned.1.call-start
  450.6 64.2 %reduce-scatter.17.cloned.1.call-done = f32[2,32,512]{2,1,0:T(8,128)} async-done(((f32[2,512,512]{2,1,0:T(8,128)}), f32[2,32,512]{2,1,0:T(8,128)}) %reduce-scatter.17.cloned.1.call-update) | async-done | bytes 131088 | tf_op jit(solution)/shard_map/reduce_scatter | solution.py:44
  514.9 2.0 fusion.63
  516.9 1.1 copy.68
  518.0 1.8 copy.70
  519.8 1.8 copy.72
  521.6 1.3 fusion.65
  522.9 2.6 fusion.8
  525.5 1.1 copy.23
  526.6 30.7 %all-gather.16.cloned.1.call-done = f32[2,512,512]{2,1,0:T(8,128)} async-done(((f32[2,32,512]{2,1,0:T(8,128)}), f32[2,512,512]{2,1,0:T(8,128)}) %all-gather.16.cloned.1.call-update) | async-done | bytes 2097168 | tf_op jit(solution)/shard_map/all_gather | solution.py:59
  557.3 2.1 fusion
  559.4 40.3 %all-gather.18.cloned.1.call-done = f32[2,512,512]{2,1,0:T(8,128)} async-done(((f32[2,32,512]{2,1,0:T(8,128)}), f32[2,512,512]{2,1,0:T(8,128)}) %all-gather.18.cloned.1.call-update) | async-done | bytes 2097168 | tf_op jit(solution)/shard_map/all_gather | solution.py:57
  599.7 2.1 fusion.1
  601.9 40.2 %all-gather.20.cloned.1.call-done = f32[2,512,512]{2,1,0:T(8,128)} async-done(((f32[2,32,512]{2,1,0:T(8,128)}), f32[2,512,512]{2,1,0:T(8,128)}) %all-gather.20.cloned.1.call-update) | async-done | bytes 2097168 | tf_op jit(solution)/shard_map/all_gather | solution.py:58
  642.0 2.1 fusion.2
  644.1 40.3 %all-gather.22.cloned.1.call-done = f32[2,512,512]{2,1,0:T(8,128)} async-done(((f32[2,32,512]{2,1,0:T(8,128)}), f32[2,512,512]{2,1,0:T(8,128)}) %all-gather.22.cloned.1.call-update) | async-done | bytes 2097168 | tf_op jit(solution)/shard_map/all_gather | solution.py:59
  684.4 42.3 %all-gather.24.cloned.1.call-done = f32[2,512,512]{2,1,0:T(8,128)} async-done(((f32[2,32,512]{2,1,0:T(8,128)}), f32[2,512,512]{2,1,0:T(8,128)}) %all-gather.24.cloned.1.call-update) | async-done | bytes 2097168 | tf_op jit(solution)/shard_map/all_gather | solution.py:57
  726.7 42.3 %all-gather.26.cloned.1.call-done = f32[2,512,512]{2,1,0:T(8,128)} async-done(((f32[2,32,512]{2,1,0:T(8,128)}), f32[2,512,512]{2,1,0:T(8,128)}) %all-gather.26.cloned.1.call-update) | async-done | bytes 2097168 | tf_op jit(solution)/shard_map/all_gather | solution.py:58
  769.0 7.4 multiply_reduce_fusion
  776.6 1.5 convolution_bitcast_fusion.1
  778.0 4.1 convolution_convert_fusion
  782.2 3.1 convolution_bitcast_fusion.3
  785.3 4.2 convolution_convert_fusion.1
  789.5 1.0 pad_maximum_fusion
  790.6 1.2 copy.48
  (54 shorter events, 0.6 us)
Async XLA Ops:
  6.5 3.5 copy-start.9
  6.5 43.6 %all-gather.10.cloned.1.call-start = ((), (), s32[]{:S(2)}) async-start(), calls=%async_computation.6 | async-start | bytes 1114112 | tf_op jit(solution)/shard_map/all_gather | solution.py:74
  7.3 81.9 %all-gather.12.cloned.1.call-start = ((), (), s32[]{:S(2)}) async-start(), calls=%async_computation.7 | async-start | bytes 1114112 | tf_op jit(solution)/shard_map/all_gather | solution.py:75
  8.0 120.2 %all-gather.14.cloned.1.call-start = ((), (), s32[]{:S(2)}) async-start(), calls=%async_computation.8 | async-start | bytes 1114112 | tf_op jit(solution)/shard_map/all_gather | solution.py:76
  8.7 1.9 copy-start.12
  8.8 183.9 %reduce-scatter.7.cloned.1.call-start = ((), (), s32[]{:S(2)}) async-start(), calls=%async_computation.9 | async-start | bytes 2228224 | tf_op jit(solution)/shard_map/reduce_scatter | solution.py:45
  92.8 164.2 %reduce-scatter.9.cloned.1.call-start = ((), (), s32[]{:S(2)}) async-start(), calls=%async_computation.11 | async-start | bytes 2228224 | tf_op jit(solution)/shard_map/reduce_scatter | solution.py:43
  131.7 189.6 %reduce-scatter.11.cloned.1.call-start = ((), (), s32[]{:S(2)}) async-start(), calls=%async_computation.13 | async-start | bytes 2228224 | tf_op jit(solution)/shard_map/reduce_scatter | solution.py:44
  133.6 1.5 copy-start
  133.6 2.0 copy-start.1
  133.6 252.3 %reduce-scatter.13.cloned.1.call-start = ((), (), s32[]{:S(2)}) async-start(), calls=%async_computation.15 | async-start | bytes 2228224 | tf_op jit(solution)/shard_map/reduce_scatter | solution.py:45
  135.1 1.8 copy-start.8
  135.6 0.8 copy-start.3
  136.1 0.8 copy-start.5
  136.9 2.0 copy-start.2
  138.8 311.6 %reduce-scatter.15.cloned.1.call-start = ((), (), s32[]{:S(2)}) async-start(), calls=%async_computation.17 | async-start | bytes 2228224 | tf_op jit(solution)/shard_map/reduce_scatter | solution.py:43
  138.9 2.3 copy-start.4
  138.9 2.3 copy-start.6
  140.4 0.8 copy-start.7
  143.1 371.7 %reduce-scatter.17.cloned.1.call-start = ((), (), s32[]{:S(2)}) async-start(), calls=%async_computation.19 | async-start | bytes 2228224 | tf_op jit(solution)/shard_map/reduce_scatter | solution.py:44
  146.2 411.1 %all-gather.16.cloned.1.call-start = ((), (), s32[]{:S(2)}) async-start(), calls=%async_computation.10 | async-start | bytes 2228224 | tf_op jit(solution)/shard_map/all_gather | solution.py:59
  192.7 407.1 %all-gather.18.cloned.1.call-start = ((), (), s32[]{:S(2)}) async-start(), calls=%async_computation.12 | async-start | bytes 2228224 | tf_op jit(solution)/shard_map/all_gather | solution.py:57
  257.0 385.0 %all-gather.20.cloned.1.call-start = ((), (), s32[]{:S(2)}) async-start(), calls=%async_computation.14 | async-start | bytes 2228224 | tf_op jit(solution)/shard_map/all_gather | solution.py:58
  321.4 363.1 %all-gather.22.cloned.1.call-start = ((), (), s32[]{:S(2)}) async-start(), calls=%async_computation.16 | async-start | bytes 2228224 | tf_op jit(solution)/shard_map/all_gather | solution.py:59
  385.9 340.8 %all-gather.24.cloned.1.call-start = ((), (), s32[]{:S(2)}) async-start(), calls=%async_computation.18 | async-start | bytes 2228224 | tf_op jit(solution)/shard_map/all_gather | solution.py:57
  450.4 318.6 %all-gather.26.cloned.1.call-start = ((), (), s32[]{:S(2)}) async-start(), calls=%async_computation.20 | async-start | bytes 2228224 | tf_op jit(solution)/shard_map/all_gather | solution.py:58
  601.8 167.2 %copy-start.13 = (f32[2]{0:T(128)S(1)}, f32[2]{0:T(128)}, u32[]{:S(2)}) copy-start(f32[2]{0:T(128)} %param.15) | copy-start | bytes 28
  769.0 7.6 copy-start.10
  785.3 4.2 copy-start.11
Sparse Core Ops, SparseCore 0:
  9.5 40.5 all-gather.9
  52.3 36.8 all-gather.11
  91.4 36.8 all-gather.13
  131.8 60.7 reduce-scatter.6
  196.2 60.7 reduce-scatter.8
  260.6 60.7 reduce-scatter.10
  325.1 60.7 reduce-scatter.12
  389.6 60.7 reduce-scatter.14
  454.1 60.6 reduce-scatter.16
  516.9 40.3 all-gather.15
  559.5 40.1 all-gather.17
  601.8 40.1 all-gather.19
  644.2 40.1 all-gather.21
  686.5 40.1 all-gather.23
  728.7 40.1 all-gather.25
where the time goes:
time: 799 us; the launch traced here: 798 us
  waiting for transfers between devices  719 us (90%)
  matrix products  36.7 us (5%)
  other arithmetic  14.9 us (2%)
  local copies, waits for them, and re-layouts  13.7 us (2%)
  between operations  13.6 us (2%)
    reduce_scatter x2, waiting for transfers between devices, summed_steps(): lax.psum_scatter(terms[0], 'tok', scatter_dimension=1, tiled=True)  129 us
    reduce_scatter x2, waiting for transfers between devices, summed_steps(): lax.psum_scatter(terms[1], 'tok', scatter_dimension=1, tiled=True)  128 us
    reduce_scatter x2, waiting for transfers between devices, summed_steps(): lax.psum_scatter(terms[2], 'tok', scatter_dimension=1, tiled=True)  111 us
    all_gather x2, waiting for transfers between devices, full_steps(): lax.all_gather(owned[0], 'tok', axis=1, tiled=True)  82.6 us
    all_gather x2, waiting for transfers between devices, full_steps(): lax.all_gather(owned[1], 'tok', axis=1, tiled=True)  82.4 us
    all_gather x2, waiting for transfers between devices, full_steps(): lax.all_gather(owned[2], 'tok', axis=1, tiled=True)  71 us
    all_gather x1, waiting for transfers between devices, shards(): lax.all_gather(fast_first, 'tok', axis=1, tiled=True)  39.5 us
    all_gather x1, waiting for transfers between devices, shards(): lax.all_gather(fast_third, 'tok', axis=1, tiled=True)  37.3 us
  transfers between devices with their start and end apart: 15, of which 15 were waited for; matrix products, arithmetic and copies ran while one was open for 5% of the time, Pallas kernels for 0%

commit v1 on v0

v1 whole, which is shorter than its diff:
```python
import functools

import jax
import jax.numpy as jnp
from jax import lax
from jax.experimental import pallas as pl
from jax.experimental.pallas import tpu as pltpu
from jax.sharding import PartitionSpec as P

MESH = pl.DeviceIdType.MESH


def forward_parts(weights, inputs):
    first, third, second = weights
    length = inputs.shape[0]
    head_count = first.shape[0]
    shaped = inputs.reshape(length, head_count, -1)
    pre_gate = jnp.einsum("thd,hfd->htf", shaped, first, preferred_element_type=jnp.float32)
    pre_up = jnp.einsum("thd,hfd->htf", shaped, third, preferred_element_type=jnp.float32)
    hidden = (jax.nn.silu(pre_gate) * pre_up).astype(jnp.bfloat16)
    return (shaped, pre_gate, pre_up, hidden)


def apply_block(weights, inputs):
    shaped, pre_gate, pre_up, hidden = forward_parts(weights, inputs)
    result = jnp.einsum("htf,hdf->thd", hidden, weights[2], preferred_element_type=jnp.float32)
    return result.reshape(inputs.shape[0], -1).astype(jnp.bfloat16)


def partial_steps(weights, keys, values, rates):
    shaped, pre_gate, pre_up, hidden = forward_parts(weights, keys)
    length = keys.shape[0]
    head_count = weights[0].shape[0]
    scaled = (
        rates[:, :, None] * values.reshape(length, head_count, -1).astype(jnp.float32)
    ).astype(jnp.bfloat16)
    step_second = jnp.einsum("thd,htf->hdf", scaled, hidden, preferred_element_type=jnp.float32)
    back = jnp.einsum("thd,hdf->htf", scaled, weights[2], preferred_element_type=jnp.float32)
    sig_gate = jax.nn.sigmoid(pre_gate)
    d_gate = (back * pre_up * sig_gate * (1.0 + pre_gate * (1.0 - sig_gate))).astype(jnp.bfloat16)
    d_up = (back * pre_gate * sig_gate).astype(jnp.bfloat16)
    step_first = jnp.einsum("htf,thd->hfd", d_gate, shaped, preferred_element_type=jnp.float32)
    step_third = jnp.einsum("htf,thd->hfd", d_up, shaped, preferred_element_type=jnp.float32)
    return (step_first, step_third, step_second)


def renorm(old, moved):
    old_norm = jnp.sqrt(jnp.sum(old * old, axis=-1, keepdims=True) + 1e-06)
    moved_norm = jnp.sqrt(jnp.sum(moved * moved, axis=-1, keepdims=True) + 1e-06)
    return moved * old_norm / moved_norm


def shards(
    query_tokens,
    key_tokens,
    value_tokens,
    learn_rates,
    fast_first,
    fast_third,
    fast_second,
    momentum_decay,
):
    owned_zero = jnp.stack([fast_first, fast_third, fast_second])
    full_zero = lax.all_gather(owned_zero, "tok", axis=2, tiled=True)
    terms_zero = partial_steps(full_zero, key_tokens[0], value_tokens[0], learn_rates[0])
    terms_one = partial_steps(full_zero, key_tokens[1], value_tokens[1], learn_rates[1])
    step_zero = lax.psum_scatter(
        jnp.stack(terms_zero).astype(jnp.bfloat16), "tok", scatter_dimension=2, tiled=True
    ).astype(jnp.float32)
    step_one = lax.psum_scatter(
        jnp.stack(terms_one).astype(jnp.bfloat16), "tok", scatter_dimension=2, tiled=True
    ).astype(jnp.float32)
    out_zero = apply_block(full_zero, query_tokens[0])
    decay = momentum_decay[None, :, None, None]
    weights_zero = owned_zero.astype(jnp.float32)
    weights_one = renorm(weights_zero, weights_zero + step_zero)
    full_one = lax.all_gather(weights_one.astype(jnp.bfloat16), "tok", axis=2, tiled=True)
    weights_two = renorm(weights_one, weights_one + decay * step_zero + step_one)
    full_two = lax.all_gather(weights_two.astype(jnp.bfloat16), "tok", axis=2, tiled=True)
    out_one = apply_block(full_one, query_tokens[1])
    out_two = apply_block(full_two, query_tokens[2])
    return jnp.stack([out_zero, out_one, out_two])


def dot_nt(a, b):
    return lax.dot_general(a, b, (((1,), (1,)), ((), ())), preferred_element_type=jnp.float32)


def dot_nn(a, b):
    return lax.dot_general(a, b, (((1,), (0,)), ((), ())), preferred_element_type=jnp.float32)


def dot_tn(a, b):
    return lax.dot_general(a, b, (((0,), (0,)), ((), ())), preferred_element_type=jnp.float32)


def kernel(
    chips,
    query_ref,
    key_ref,
    value_ref,
    rate_ref,
    first_ref,
    third_ref,
    second_ref,
    decay_ref,
    out_ref,
    queries,
    keys,
    values,
    rates,
    full,
    part,
    stage,
    landed,
    step_own,
    weight_own,
    result,
    gates,
    ups,
    hiddens,
    swap_send,
    swap_recv,
    local_sem,
    gather_send,
    gather_recv,
    sum_send,
    sum_recv,
    out_send,
    out_recv,
    out_local,
):
    index = lax.axis_index("tok")
    chip = index // 2
    core = index % 2
    odd = chip % 2
    place = (1 - odd) * (chip // 2) + odd * (chips - 1 - chip // 2)
    half = chips // 2

    def chip_at(position):
        wrapped = (position + chips) % chips
        back = wrapped // half
        return (1 - back) * (2 * wrapped) + back * (2 * (chips - 1 - wrapped) + 1)

    partner = {"tok": index + 1 - 2 * core}
    sides = (
        {"tok": 2 * chip_at(place + 1) + core},
        {"tok": 2 * chip_at(place - 1) + core},
    )
    rows = first_ref.shape[1]
    block = 2 * rows
    tokens = key_ref.shape[1]
    width = first_ref.shape[2]
    cut = width // 2

    barrier = pltpu.get_barrier_semaphore()
    for other in (partner,) + sides:
        pl.semaphore_signal(barrier, inc=1, device_id=other, device_id_type=MESH)
    pl.semaphore_wait(barrier, 3)

    mine = pl.ds(pl.multiple_of(core * width, width), width)
    theirs = pl.ds(pl.multiple_of((1 - core) * width, width), width)
    slot = pl.ds(pl.multiple_of(core * tokens, tokens), tokens)
    other_slot = pl.ds(pl.multiple_of((1 - core) * tokens, tokens), tokens)
    shard = pl.ds(pl.multiple_of(index * rows, rows), rows)

    pairs = []
    for m, ref in enumerate((first_ref, third_ref, second_ref)):
        pairs.append((ref.at[1 - core], ref.at[core], full.at[0, m, shard, :]))
    for b in range(2):
        pairs.append((key_ref.at[b, :, theirs], key_ref.at[b, :, mine], keys.at[b, slot, :]))
        pairs.append((value_ref.at[b, :, theirs], value_ref.at[b, :, mine], values.at[b, slot, :]))
        pairs.append((rate_ref.at[b], rate_ref.at[b], rates.at[b, slot, :]))
    for b in range(3):
        pairs.append((query_ref.at[b, :, theirs], query_ref.at[b, :, mine], queries.at[b, slot, :]))
    swaps = []
    locals_ = []
    for n, (away, here, target) in enumerate(pairs):
        swap = pltpu.make_async_remote_copy(
            src_ref=away,
            dst_ref=target,
            send_sem=swap_send.at[n],
            recv_sem=swap_recv.at[n],
            device_id=partner,
            device_id_type=MESH,
        )
        swap.start()
        kept = pltpu.make_async_copy(here, target, local_sem.at[n])
        kept.start()
        swaps.append(swap)
        locals_.append(kept)

    def ready(n):
        swaps[n].wait_recv()
        locals_[n].wait()

    def rows_of(owner):
        return pl.ds(pl.multiple_of(owner * block, block), block)

    def cols_of(way):
        return pl.ds(way * cut, cut)

    sent = []

    def gather_copy(k, m, way, s):
        owner = chip_at(place - (s - 1)) if way == 0 else chip_at(place + (s - 1))
        span = full.at[k, m, rows_of(owner), cols_of(way) if s == half else pl.ds(0, width)]
        return pltpu.make_async_remote_copy(
            src_ref=span,
            dst_ref=span,
            send_sem=gather_send.at[k, m, way, s - 1],
            recv_sem=gather_recv.at[k, m, way, s - 1],
            device_id=sides[way],
            device_id_type=MESH,
        )

    def gather_start(k, m, way, s):
        copy = gather_copy(k, m, way, s)
        copy.start()
        sent.append(copy)

    def gather_step(k, s, order=(0, 1, 2)):
        for m in order:
            for way in range(2):
                gather_copy(k, m, way, s).wait_recv()
                if s < half:
                    gather_start(k, m, way, s + 1)

    def sum_copy(t, way, s):
        span = cols_of(way) if s == 1 else pl.ds(0, width)
        return pltpu.make_async_remote_copy(
            src_ref=stage.at[t, way, s - 1, :, span],
            dst_ref=landed.at[t, way, s - 1, :, span],
            send_sem=sum_send.at[t, way, s - 1],
            recv_sem=sum_recv.at[t, way, s - 1],
            device_id=sides[way],
            device_id_type=MESH,
        )

    def sum_start(t, way, s):
        ahead = half - s + 1
        owner = chip_at(place + ahead) if way == 0 else chip_at(place - ahead)
        span = cols_of(way)
        if s == 1:
            stage[t, way, 0, :, span] = part[t, rows_of(owner), span].astype(jnp.bfloat16)
        elif s == 2:
            rest = cols_of(1 - way)
            stage[t, way, 1, :, span] = (
                part[t, rows_of(owner), span] + landed[t, way, 0, :, span].astype(jnp.float32)
            ).astype(jnp.bfloat16)
            stage[t, way, 1, :, rest] = part[t, rows_of(owner), rest].astype(jnp.bfloat16)
        else:
            stage[t, way, s - 1] = (
                part[t, rows_of(owner), :] + landed[t, way, s - 2].astype(jnp.float32)
            ).astype(jnp.bfloat16)
        copy = sum_copy(t, way, s)
        copy.start()
        sent.append(copy)

    order = (2, 0, 1)

    def sum_step(j, s):
        for m in order:
            for way in range(2):
                sum_copy(3 * j + m, way, s).wait_recv()
                sum_start(3 * j + m, way, s + 1)

    def total_of(t):
        for way in range(2):
            sum_copy(t, way, half).wait_recv()
        own = part[t, rows_of(chip), :]
        return (
            own
            + landed[t, 0, half - 1].astype(jnp.float32)
            + landed[t, 1, half - 1].astype(jnp.float32)
        )

    def forward(k, x):
        gate = dot_nt(x, full[k, 0])
        up = dot_nt(x, full[k, 1])
        sig = jax.nn.sigmoid(gate)
        return gate, up, sig, (gate * sig * up).astype(jnp.bfloat16)

    def keys_forward(j):
        gate, up, sig, hidden = forward(0, keys[j])
        gates[...] = gate
        ups[...] = up
        hiddens[...] = hidden

    def steps(j):
        rate = jnp.where(core == 0, rates[j, :, 0:1], rates[j, :, 1:2])
        scaled = (rate * values[j].astype(jnp.float32)).astype(jnp.bfloat16)
        part[3 * j + 2] = dot_tn(scaled, hiddens[...])
        for way in range(2):
            sum_start(3 * j + 2, way, 1)
        back = dot_nn(scaled, full[0, 2])
        gate = gates[...]
        sig = jax.nn.sigmoid(gate)
        x = keys[j]
        d_gate = (back * ups[...] * sig * (1.0 + gate * (1.0 - sig))).astype(jnp.bfloat16)
        part[3 * j] = dot_tn(d_gate, x)
        for way in range(2):
            sum_start(3 * j, way, 1)
        d_up = (back * gate * sig).astype(jnp.bfloat16)
        part[3 * j + 1] = dot_tn(d_up, x)
        for way in range(2):
            sum_start(3 * j + 1, way, 1)

    outs = []

    def read_hidden(k):
        gate, up, sig, hidden = forward(k, queries[k])
        hiddens[...] = hidden

    def read_out(k):
        result[k] = dot_nt(hiddens[...], full[k, 2]).astype(jnp.bfloat16)
        away = pltpu.make_async_remote_copy(
            src_ref=result.at[k, other_slot, :],
            dst_ref=out_ref.at[k, :, mine],
            send_sem=out_send.at[k],
            recv_sem=out_recv.at[k],
            device_id=partner,
            device_id_type=MESH,
        )
        away.start()
        here = pltpu.make_async_copy(
            result.at[k, slot, :], out_ref.at[k, :, mine], out_local.at[k]
        )
        here.start()
        outs.append((away, here))

    for m in range(3):
        ready(m)
        for way in range(2):
            gather_start(0, m, way, 1)
    for s in range(1, half + 1):
        gather_step(0, s)

    for n in range(3, len(pairs)):
        ready(n)
    keys_forward(0)
    steps(0)
    keys_forward(1)
    sum_step(0, 1)
    steps(1)
    later = [functools.partial(read_hidden, 0), functools.partial(read_out, 0)]
    for s in range(2, half):
        sum_step(0, s)
        sum_step(1, s - 1)
        if s == 2:
            for piece in later:
                piece()
    decay = decay_ref[core]
    for m in order:
        moment = total_of(m)
        step_own[m] = moment
        old = full[0, m, rows_of(chip), :].astype(jnp.float32)
        fresh = renorm(old, old + moment)
        weight_own[m] = fresh
        full[1, m, rows_of(chip), :] = fresh.astype(jnp.bfloat16)
        for way in range(2):
            gather_start(1, m, way, 1)
    sum_step(1, half - 1)
    gather_step(1, 1, order)
    for m in order:
        moment = decay * step_own[m] + total_of(3 + m)
        old = weight_own[m]
        fresh = renorm(old, old + moment)
        full[2, m, rows_of(chip), :] = fresh.astype(jnp.bfloat16)
        for way in range(2):
            gather_start(2, m, way, 1)
    for s in range(2, half + 1):
        gather_step(1, s, order)
        if s < half:
            gather_step(2, s - 1, (0, 1, 2))
    read_hidden(1)
    read_out(1)
    gather_step(2, half - 1, (0, 1, 2))
    gather_step(2, half, (0, 1))
    read_hidden(2)
    gather_step(2, half, (2,))
    read_out(2)

    for n in range(len(pairs)):
        swaps[n].wait_send()
    for copy in sent:
        copy.wait_send()
    for away, here in outs:
        here.wait()
        away.wait()


def fused_shards(chips, query, key, value, rate, first, third, second, decay):
    blocks, tokens, features = query.shape
    heads, rows, width = first.shape
    half = chips // 2
    hidden = 2 * rows * chips
    span = 2 * tokens
    anywhere = pl.BlockSpec(memory_space=pl.ANY)
    dma = pltpu.SemaphoreType.DMA
    low, wide = jnp.bfloat16, jnp.float32
    return pl.pallas_call(
        functools.partial(kernel, chips),
        out_shape=jax.ShapeDtypeStruct(query.shape, low),
        in_specs=[anywhere] * 7 + [pl.BlockSpec(memory_space=pltpu.SMEM)],
        out_specs=anywhere,
        scratch_shapes=[
            pltpu.VMEM((3, span, width), low),
            pltpu.VMEM((2, span, width), low),
            pltpu.VMEM((2, span, width), low),
            pltpu.VMEM((2, span, heads), wide),
            pltpu.VMEM((3, 3, hidden, width), low),
            pltpu.VMEM((6, hidden, width), wide),
            pltpu.VMEM((6, 2, half, 2 * rows, width), low),
            pltpu.VMEM((6, 2, half, 2 * rows, width), low),
            pltpu.VMEM((3, 2 * rows, width), wide),
            pltpu.VMEM((3, 2 * rows, width), wide),
            pltpu.VMEM((3, span, width), low),
            pltpu.VMEM((span, hidden), wide),
            pltpu.VMEM((span, hidden), wide),
            pltpu.VMEM((span, hidden), low),
            dma((12,)),
            dma((12,)),
            dma((12,)),
            dma((3, 3, 2, half)),
            dma((3, 3, 2, half)),
            dma((6, 2, half)),
            dma((6, 2, half)),
            dma((3,)),
            dma((3,)),
            dma((3,)),
        ],
        compiler_params=pltpu.CompilerParams(
            collective_id=0, has_side_effects=True, vmem_limit_bytes=60 * 1024 * 1024
        ),
    )(query, key, value, rate, first, third, second, decay)


def solution(mesh):
    placed = (
        P(None, ("groups", "tok"), None),
        P(None, ("groups", "tok"), None),
        P(None, ("groups", "tok"), None),
        P(None, ("groups", "tok"), None),
        P(None, "tok", None),
        P(None, "tok", None),
        P(None, "tok", None),
        P(),
    )
    chips = mesh.shape["tok"] // 2

    def body(*arrays):
        rows = arrays[4].shape[1]
        if rows % 16 or chips % 2 or chips < 4:
            return shards(*arrays)
        return fused_shards(chips, *arrays)

    return jax.shard_map(
        body,
        mesh=mesh,
        in_specs=placed,
        out_specs=P(None, ("groups", "tok"), None),
        check_vma=False,
    )
```

time: 799 us -> 95.3 us (0.12)
  waiting for transfers between devices: 719 us -> 0 us
  Pallas kernels: 0 us -> 91.5 us
  matrix products: 36.7 us -> 0 us
  other arithmetic: 14.9 us -> 0 us
  between operations: 13.6 us -> 0.01 us
  local copies, waits for them, and re-layouts: 13.7 us -> 3.57 us
    reduce_scatter x6 -> x0, waiting for transfers between devices: 368 us -> none  [the longest x2 129 us: summed_steps(): lax.psum_scatter(terms[0], 'tok', scatter_dimension=1, tiled=True)]
    all_gather x9 -> x0, waiting for transfers between devices: 348 us -> none  [the longest x2 82.6 us: full_steps(): lax.all_gather(owned[0], 'tok', axis=1, tiled=True)]
    pallas_call x0 -> x1, Pallas kernels: none -> 91.5 us  [fused_shards(): pl.pallas_call(functools.partial(kernel, chips), out_shape=jax.ShapeDtype...]
    dot_general x18 -> x0, matrix products: 36.7 us -> none  [the longest x3 11 us: apply_block(): jnp.einsum('htf,hdf->thd', hidden, weights[2], preferred_element_type=jnp...]
    reduce_sum x4 -> x0, other arithmetic: 13.7 us -> none  [the longest x1 7.45 us: renorm(): jnp.sum(moved * moved, axis=-1, keepdims=True) + 1e-06]
  transfers between devices with their start and end apart: 15 -> 0, of which waited for: 15 -> 0; matrix products, arithmetic and copies ran while one was open for 5% -> 0% of each run, Pallas kernels for 0% -> 0%
where the time goes in v1:
time: 95.3 us; the launch traced here: 95.1 us
  Pallas kernels  91.5 us (96%)
  local copies, waits for them, and re-layouts  3.57 us (4%)
    pallas_call x1, Pallas kernels, fused_shards(): pl.pallas_call(functools.partial(kernel, chips), out_shape=jax.ShapeDtype...  91.5 us
    unnamed x2, local copies, waits for them, and re-layouts  3.57 us

profile of v1, /device:TPU:0, one launch (start us, length us, event | category | flops | bytes accessed | tf_op | source)
XLA Modules:
  0.0 95.1 jit_solution(10241908022493875425)
XLA Ops:
  0.0 1.5 %copy.9.rate_ref = f32[3,128,2]{2,1,0:T(8,128)} copy(f32[3,128,2]{1,2,0:T(2,128)} %param.11) | data formatting | bytes 6144 | tf_op args[3]
  1.5 91.5 %shard_map.82 = bf16[3,128,1024]{2,1,0:T(8,128)(2,1)} custom-call(bf16[3,128,1024]{2,1,0:T(8,128)(2,1)} %query_ref.1, bf16[3,128,1024]{2,1,0:T(8,128)(2,1)} %key_ref.1, bf16[3,128,1024]{2,1,0:T(8,128)(2,1)} %value_ref.1, f32[3,128,2]{2,1,0:T(8,128)} %copy.9.rate_ref, bf16[2,32,512]{2,1,0:T(8,128)(2,1)} %first_ref.1, bf16[2,32,512]{2,1,0:T(8,128)(2,1)} %third_ref.1, ...), custom_call_target="tpu_custom_call" | custom-call | tf_op jit(solution)/shard_map/pallas_call | solution.py:402
  93.0 2.1 %copy.11 = bf16[3,128,1024]{2,1,0:T(8,128)(2,1)} copy(bf16[3,128,1024]{2,1,0:T(8,128)(2,1)} %shard_map.82) | data formatting | bytes 1572864

commit v2 on v1

v2 whole, which is shorter than its diff:
```python
import jax
import jax.numpy as jnp
from jax import lax
from jax.experimental import pallas as pl
from jax.experimental.pallas import tpu as pltpu
from jax.sharding import PartitionSpec as P

MESH = pl.DeviceIdType.MESH


def forward_parts(weights, inputs):
    first, third, second = weights
    length = inputs.shape[0]
    head_count = first.shape[0]
    shaped = inputs.reshape(length, head_count, -1)
    pre_gate = jnp.einsum("thd,hfd->htf", shaped, first, preferred_element_type=jnp.float32)
    pre_up = jnp.einsum("thd,hfd->htf", shaped, third, preferred_element_type=jnp.float32)
    hidden = (jax.nn.silu(pre_gate) * pre_up).astype(jnp.bfloat16)
    return (shaped, pre_gate, pre_up, hidden)


def apply_block(weights, inputs):
    shaped, pre_gate, pre_up, hidden = forward_parts(weights, inputs)
    result = jnp.einsum("htf,hdf->thd", hidden, weights[2], preferred_element_type=jnp.float32)
    return result.reshape(inputs.shape[0], -1).astype(jnp.bfloat16)


def partial_steps(weights, keys, values, rates):
    shaped, pre_gate, pre_up, hidden = forward_parts(weights, keys)
    length = keys.shape[0]
    head_count = weights[0].shape[0]
    scaled = (
        rates[:, :, None] * values.reshape(length, head_count, -1).astype(jnp.float32)
    ).astype(jnp.bfloat16)
    step_second = jnp.einsum("thd,htf->hdf", scaled, hidden, preferred_element_type=jnp.float32)
    back = jnp.einsum("thd,hdf->htf", scaled, weights[2], preferred_element_type=jnp.float32)
    sig_gate = jax.nn.sigmoid(pre_gate)
    d_gate = (back * pre_up * sig_gate * (1.0 + pre_gate * (1.0 - sig_gate))).astype(jnp.bfloat16)
    d_up = (back * pre_gate * sig_gate).astype(jnp.bfloat16)
    step_first = jnp.einsum("htf,thd->hfd", d_gate, shaped, preferred_element_type=jnp.float32)
    step_third = jnp.einsum("htf,thd->hfd", d_up, shaped, preferred_element_type=jnp.float32)
    return (step_first, step_third, step_second)


def renorm(old, moved):
    old_norm = jnp.sqrt(jnp.sum(old * old, axis=-1, keepdims=True) + 1e-06)
    moved_norm = jnp.sqrt(jnp.sum(moved * moved, axis=-1, keepdims=True) + 1e-06)
    return moved * old_norm / moved_norm


def shards(
    query_tokens,
    key_tokens,
    value_tokens,
    learn_rates,
    fast_first,
    fast_third,
    fast_second,
    momentum_decay,
):
    owned_zero = jnp.stack([fast_first, fast_third, fast_second])
    full_zero = lax.all_gather(owned_zero, "tok", axis=2, tiled=True)
    terms_zero = partial_steps(full_zero, key_tokens[0], value_tokens[0], learn_rates[0])
    terms_one = partial_steps(full_zero, key_tokens[1], value_tokens[1], learn_rates[1])
    step_zero = lax.psum_scatter(
        jnp.stack(terms_zero).astype(jnp.bfloat16), "tok", scatter_dimension=2, tiled=True
    ).astype(jnp.float32)
    step_one = lax.psum_scatter(
        jnp.stack(terms_one).astype(jnp.bfloat16), "tok", scatter_dimension=2, tiled=True
    ).astype(jnp.float32)
    out_zero = apply_block(full_zero, query_tokens[0])
    decay = momentum_decay[None, :, None, None]
    weights_zero = owned_zero.astype(jnp.float32)
    weights_one = renorm(weights_zero, weights_zero + step_zero)
    full_one = lax.all_gather(weights_one.astype(jnp.bfloat16), "tok", axis=2, tiled=True)
    weights_two = renorm(weights_one, weights_one + decay * step_zero + step_one)
    full_two = lax.all_gather(weights_two.astype(jnp.bfloat16), "tok", axis=2, tiled=True)
    out_one = apply_block(full_one, query_tokens[1])
    out_two = apply_block(full_two, query_tokens[2])
    return jnp.stack([out_zero, out_one, out_two])


def dot_nt(a, b):
    return lax.dot_general(a, b, (((1,), (1,)), ((), ())), preferred_element_type=jnp.float32)


def dot_nn(a, b):
    return lax.dot_general(a, b, (((1,), (0,)), ((), ())), preferred_element_type=jnp.float32)


def dot_tn(a, b):
    return lax.dot_general(a, b, (((0,), (0,)), ((), ())), preferred_element_type=jnp.float32)


def kernel(
    query_ref,
    key_ref,
    value_ref,
    rate_ref,
    first_ref,
    third_ref,
    second_ref,
    decay_ref,
    out_ref,
    queries,
    keys,
    values,
    rates,
    full,
    part,
    core_out,
    core_in,
    side_out,
    side_in,
    far_out,
    far_in,
    step_own,
    weight_own,
    result,
    gates,
    ups,
    hiddens,
    swap_send,
    swap_recv,
    local_sem,
    gather_send,
    gather_recv,
    sum_send,
    sum_recv,
    out_send,
    out_recv,
    out_local,
):
    index = lax.axis_index("tok")
    core = index % 2
    lane = (index // 2) % 2
    head = (index // 4) % 2
    pair = index // 8
    partner = {"tok": index + 1 - 2 * core}
    beside = {"tok": index + 2 - 4 * lane}
    mate = {"tok": index + 4 - 8 * head}
    beyond = {"tok": index + 8 - 16 * pair}
    rows = first_ref.shape[1]
    tokens = key_ref.shape[1]
    width = first_ref.shape[2]
    hidden_units = 16 * rows

    barrier = pltpu.get_barrier_semaphore()
    for other in (partner, beside, mate, beyond):
        pl.semaphore_signal(barrier, inc=1, device_id=other, device_id_type=MESH)
    pl.semaphore_wait(barrier, 4)

    sent = []

    def push(src, dst, send_sem, recv_sem, to):
        return pltpu.make_async_remote_copy(
            src_ref=src,
            dst_ref=dst,
            send_sem=send_sem,
            recv_sem=recv_sem,
            device_id=to,
            device_id_type=MESH,
        )

    def go(copy):
        copy.start()
        sent.append(copy)

    mine = pl.ds(pl.multiple_of(head * width, width), width)
    theirs = pl.ds(pl.multiple_of((1 - head) * width, width), width)
    slot = pl.ds(pl.multiple_of(head * tokens, tokens), tokens)
    other_slot = pl.ds(pl.multiple_of((1 - head) * tokens, tokens), tokens)

    pairs = []
    for m, ref in enumerate((first_ref, third_ref, second_ref)):
        pairs.append((ref.at[1 - head], ref.at[head], full.at[0, m, pair, head, lane, core]))
    for b in range(2):
        pairs.append((key_ref.at[b, :, theirs], key_ref.at[b, :, mine], keys.at[b, slot, :]))
        pairs.append((value_ref.at[b, :, theirs], value_ref.at[b, :, mine], values.at[b, slot, :]))
        pairs.append((rate_ref.at[b], rate_ref.at[b], rates.at[b, :, slot]))
    for b in range(3):
        pairs.append((query_ref.at[b, :, theirs], query_ref.at[b, :, mine], queries.at[b, slot, :]))
    swaps = {}
    locals_ = {}

    def swap(first, last):
        for n in range(first, last):
            away, here, target = pairs[n]
            swaps[n] = push(away, target, swap_send.at[n], swap_recv.at[n], mate)
            swaps[n].start()
            locals_[n] = pltpu.make_async_copy(here, target, local_sem.at[n])
            locals_[n].start()

    def ready(n):
        swaps[n].wait_recv()
        locals_[n].wait()

    def block_of(k, m, p, q):
        return full.at[k, m, p, :, q, core]

    def gather_copy(k, m, n):
        p, q = (
            (pair, lane),
            (pair, lane),
            (1 - pair, lane),
            (pair, lane),
            (1 - pair, lane),
            (pair, 1 - lane),
            (1 - pair, 1 - lane),
        )[n]
        span = block_of(k, m, p, q)
        to = (beyond, beside, beside, partner, partner, partner, partner)[n]
        return push(span, span, gather_send.at[k, m, n], gather_recv.at[k, m, n], to)

    def gather_own(k, m):
        for n in (0, 1, 3):
            go(gather_copy(k, m, n))

    def gather_beyond(k, m):
        gather_copy(k, m, 0).wait_recv()
        go(gather_copy(k, m, 2))
        go(gather_copy(k, m, 4))

    def gather_beside(k, m, n):
        gather_copy(k, m, n).wait_recv()
        go(gather_copy(k, m, n + 4))

    def gather_end(k, m):
        for n in range(3, 7):
            gather_copy(k, m, n).wait_recv()

    def core_copy(t):
        return push(
            core_out.at[t], core_in.at[t], sum_send.at[t, 0], sum_recv.at[t, 0], partner
        )

    def side_copy(t, p, n):
        return push(
            side_out.at[t, p], side_in.at[t, p], sum_send.at[t, n], sum_recv.at[t, n], beside
        )

    def far_copy(t):
        return push(far_out.at[t], far_in.at[t], sum_send.at[t, 3], sum_recv.at[t, 3], beyond)

    def core_start(t):
        core_out[t] = part[t, :, :, :, 1 - core].astype(jnp.bfloat16)
        go(core_copy(t))

    def core_sum(t, p, q):
        return part[t, p, :, q, core] + core_in[t, p, :, q].astype(jnp.float32)

    def side_start(t):
        core_copy(t).wait_recv()
        for n, p in ((1, 1 - pair), (2, pair)):
            side_out[t, p] = core_sum(t, p, 1 - lane).astype(jnp.bfloat16)
            go(side_copy(t, p, n))

    def far_start(t):
        p = 1 - pair
        side_copy(t, p, 1).wait_recv()
        far_out[t] = (core_sum(t, p, lane) + side_in[t, p].astype(jnp.float32)).astype(
            jnp.bfloat16
        )
        go(far_copy(t))

    def total_of(t):
        side_copy(t, pair, 2).wait_recv()
        near = core_sum(t, pair, lane) + side_in[t, pair].astype(jnp.float32)
        far_copy(t).wait_recv()
        return near + far_in[t].astype(jnp.float32)

    order = (2, 0, 1)

    def whole(k, m):
        return full[k, m].reshape(hidden_units, width)

    def forward(k, x):
        gate = dot_nt(x, whole(k, 0))
        up = dot_nt(x, whole(k, 1))
        sig = jax.nn.sigmoid(gate)
        return gate, up, sig, (gate * sig * up).astype(jnp.bfloat16)

    def keys_forward(j):
        gate, up, sig, hidden = forward(0, keys[j])
        gates[...] = gate
        ups[...] = up
        hiddens[...] = hidden

    def steps(j):
        row = jnp.where(head == 0, rates[j, 0:1, :], rates[j, 1:2, :])
        rate = jnp.transpose(jnp.broadcast_to(row, (128, row.shape[1])))[:, 0:1]
        scaled = (rate * values[j].astype(jnp.float32)).astype(jnp.bfloat16)
        part[3 * j + 2] = dot_tn(scaled, hiddens[...]).reshape(part.shape[1:])
        core_start(3 * j + 2)
        back = dot_nn(scaled, whole(0, 2))
        gate = gates[...]
        sig = jax.nn.sigmoid(gate)
        x = keys[j]
        d_gate = (back * ups[...] * sig * (1.0 + gate * (1.0 - sig))).astype(jnp.bfloat16)
        part[3 * j] = dot_tn(d_gate, x).reshape(part.shape[1:])
        core_start(3 * j)
        d_up = (back * gate * sig).astype(jnp.bfloat16)
        part[3 * j + 1] = dot_tn(d_up, x).reshape(part.shape[1:])
        core_start(3 * j + 1)

    outs = []

    def read_hidden(k):
        gate, up, sig, hidden = forward(k, queries[k])
        hiddens[...] = hidden

    def read_out(k):
        result[k] = dot_nt(hiddens[...], whole(k, 2)).astype(jnp.bfloat16)
        away = push(
            result.at[k, other_slot, :],
            out_ref.at[k, :, mine],
            out_send.at[k],
            out_recv.at[k],
            mate,
        )
        away.start()
        here = pltpu.make_async_copy(
            result.at[k, slot, :], out_ref.at[k, :, mine], out_local.at[k]
        )
        here.start()
        outs.append((away, here))

    swap(0, 6)
    for m in range(3):
        ready(m)
        gather_own(0, m)
    swap(6, 9)
    for m in range(3):
        gather_beyond(0, m)
        gather_beside(0, m, 1)
    for m in range(3):
        gather_beside(0, m, 2)
    for m in range(3):
        gather_end(0, m)
    for n in range(3, 6):
        ready(n)
    keys_forward(0)
    steps(0)
    for m in order:
        side_start(m)
    swap(9, 11)
    for n in range(6, 9):
        ready(n)
    keys_forward(1)
    steps(1)
    for m in order:
        far_start(m)
        side_start(3 + m)
    ready(9)
    read_hidden(0)
    read_out(0)
    swap(11, 12)
    for m in order:
        moment = total_of(m)
        step_own[m] = moment
        old = full[0, m, pair, :, lane, core].astype(jnp.float32)
        fresh = renorm(old, old + moment)
        weight_own[m] = fresh
        full[1, m, pair, :, lane, core] = fresh.astype(jnp.bfloat16)
        gather_own(1, m)
    decay = decay_ref[head]
    for m in order:
        far_start(3 + m)
    for m in order:
        gather_beyond(1, m)
        gather_beside(1, m, 1)
    for m in order:
        moment = decay * step_own[m] + total_of(3 + m)
        old = weight_own[m]
        fresh = renorm(old, old + moment)
        full[2, m, pair, :, lane, core] = fresh.astype(jnp.bfloat16)
        gather_own(2, m)
    for m in order:
        gather_beside(1, m, 2)
    for m in order:
        gather_beyond(2, m)
        gather_beside(2, m, 1)
    for m in range(3):
        gather_end(1, m)
    ready(10)
    ready(11)
    read_hidden(1)
    read_out(1)
    for m in order:
        gather_beside(2, m, 2)
    for m in (0, 1):
        gather_end(2, m)
    read_hidden(2)
    gather_end(2, 2)
    read_out(2)

    for n in range(len(pairs)):
        swaps[n].wait_send()
    for copy in sent:
        copy.wait_send()
    for away, here in outs:
        here.wait()
        away.wait()


def fused_shards(query, key, value, rate, first, third, second, decay):
    blocks, tokens, features = query.shape
    heads, rows, width = first.shape
    hidden = 16 * rows
    span = 2 * tokens
    anywhere = pl.BlockSpec(memory_space=pl.ANY)
    dma = pltpu.SemaphoreType.DMA
    low, wide = jnp.bfloat16, jnp.float32
    return pl.pallas_call(
        kernel,
        out_shape=jax.ShapeDtypeStruct(query.shape, low),
        in_specs=[anywhere] * 7 + [pl.BlockSpec(memory_space=pltpu.SMEM)],
        out_specs=anywhere,
        scratch_shapes=[
            pltpu.VMEM((3, span, width), low),
            pltpu.VMEM((2, span, width), low),
            pltpu.VMEM((2, span, width), low),
            pltpu.VMEM((2, heads, span), wide),
            pltpu.VMEM((3, 3, 2, 2, 2, 2, rows, width), low),
            pltpu.VMEM((6, 2, 2, 2, 2, rows, width), wide),
            pltpu.VMEM((6, 2, 2, 2, rows, width), low),
            pltpu.VMEM((6, 2, 2, 2, rows, width), low),
            pltpu.VMEM((6, 2, 2, rows, width), low),
            pltpu.VMEM((6, 2, 2, rows, width), low),
            pltpu.VMEM((6, 2, rows, width), low),
            pltpu.VMEM((6, 2, rows, width), low),
            pltpu.VMEM((3, 2, rows, width), wide),
            pltpu.VMEM((3, 2, rows, width), wide),
            pltpu.VMEM((3, span, width), low),
            pltpu.VMEM((span, hidden), wide),
            pltpu.VMEM((span, hidden), wide),
            pltpu.VMEM((span, hidden), low),
            dma((12,)),
            dma((12,)),
            dma((12,)),
            dma((3, 3, 7)),
            dma((3, 3, 7)),
            dma((6, 4)),
            dma((6, 4)),
            dma((3,)),
            dma((3,)),
            dma((3,)),
        ],
        compiler_params=pltpu.CompilerParams(
            collective_id=0, has_side_effects=True, vmem_limit_bytes=60 * 1024 * 1024
        ),
    )(query, key, value, jnp.swapaxes(rate, 1, 2), first, third, second, decay)


def solution(mesh):
    placed = (
        P(None, ("groups", "tok"), None),
        P(None, ("groups", "tok"), None),
        P(None, ("groups", "tok"), None),
        P(None, ("groups", "tok"), None),
        P(None, "tok", None),
        P(None, "tok", None),
        P(None, "tok", None),
        P(),
    )
    chips = mesh.shape["tok"] // 2

    def body(*arrays):
        rows = arrays[4].shape[1]
        if rows % 16 or chips != 8 or arrays[4].shape[0] != 2:
            return shards(*arrays)
        return fused_shards(*arrays)

    return jax.shard_map(
        body,
        mesh=mesh,
        in_specs=placed,
        out_specs=P(None, ("groups", "tok"), None),
        check_vma=False,
    )
```

time: 95.3 us -> 78 us (0.82)
  Pallas kernels: 91.5 us -> 75.7 us
  local copies, waits for them, and re-layouts: 3.57 us -> 2.06 us
    pallas_call x1, Pallas kernels: 91.5 us -> 75.7 us  [fused_shards(): pl.pallas_call(kernel, out_shape=jax.ShapeDtypeStruct(query.shape, low),...]
    unnamed x2 -> x1, local copies, waits for them, and re-layouts: 3.57 us -> 2.06 us
where the time goes in v2:
time: 78 us; the launch traced here: 77.8 us
  Pallas kernels  75.7 us (97%)
  local copies, waits for them, and re-layouts  2.06 us (3%)
    pallas_call x1, Pallas kernels, fused_shards(): pl.pallas_call(kernel, out_shape=jax.ShapeDtypeStruct(query.shape, low),...  75.7 us
    unnamed x1, local copies, waits for them, and re-layouts  2.06 us

profile of v2, /device:TPU:0, one launch (start us, length us, event | category | flops | bytes accessed | tf_op | source)
XLA Modules:
  0.0 77.8 jit_solution(16137071870993881449)
XLA Ops:
  0.0 75.7 %shard_map.82 = bf16[3,128,1024]{2,1,0:T(8,128)(2,1)} custom-call(bf16[3,128,1024]{2,1,0:T(8,128)(2,1)} %query_ref.1, bf16[3,128,1024]{2,1,0:T(8,128)(2,1)} %key_ref.1, bf16[3,128,1024]{2,1,0:T(8,128)(2,1)} %value_ref.1, f32[3,2,128]{2,1,0:T(2,128)} %bitcast.1, bf16[2,32,512]{2,1,0:T(8,128)(2,1)} %first_ref.1, bf16[2,32,512]{2,1,0:T(8,128)(2,1)} %third_ref.1, ...), custom_call_target="tpu_custom_call" | custom-call | tf_op jit(solution)/shard_map/pallas_call | solution.py:414
  75.7 2.1 %copy.10 = bf16[3,128,1024]{2,1,0:T(8,128)(2,1)} copy(bf16[3,128,1024]{2,1,0:T(8,128)(2,1)} %shard_map.82) | data formatting | bytes 1572864

commit v3 on v2

--- a/solution.py
+++ b/solution.py
@@ -325,11 +325,11 @@
         here.start()
         outs.append((away, here))
 
-    swap(0, 6)
+    swap(0, 3)
     for m in range(3):
         ready(m)
         gather_own(0, m)
-    swap(6, 9)
+    swap(3, 9)
     for m in range(3):
         gather_beyond(0, m)
         gather_beside(0, m, 1)
@@ -343,7 +343,6 @@
     steps(0)
     for m in order:
         side_start(m)
-    swap(9, 11)
     for n in range(6, 9):
         ready(n)
     keys_forward(1)
@@ -351,10 +350,7 @@
     for m in order:
         far_start(m)
         side_start(3 + m)
-    ready(9)
-    read_hidden(0)
-    read_out(0)
-    swap(11, 12)
+    swap(9, 10)
     for m in order:
         moment = total_of(m)
         step_own[m] = moment
@@ -366,6 +362,10 @@
     decay = decay_ref[head]
     for m in order:
         far_start(3 + m)
+    swap(10, 11)
+    ready(9)
+    read_hidden(0)
+    read_out(0)
     for m in order:
         gather_beyond(1, m)
         gather_beside(1, m, 1)
@@ -375,6 +375,7 @@
         fresh = renorm(old, old + moment)
         full[2, m, pair, :, lane, core] = fresh.astype(jnp.bfloat16)
         gather_own(2, m)
+    swap(11, 12)
     for m in order:
         gather_beside(1, m, 2)
     for m in order:
@@ -383,15 +384,18 @@
     for m in range(3):
         gather_end(1, m)
     ready(10)
-    ready(11)
     read_hidden(1)
     read_out(1)
+    ready(11)
     for m in order:
         gather_beside(2, m, 2)
-    for m in (0, 1):
-        gather_end(2, m)
-    read_hidden(2)
     gather_end(2, 2)
+    gather_end(2, 0)
+    gates[...] = dot_nt(queries[2], whole(2, 0))
+    gather_end(2, 1)
+    gate = gates[...]
+    up = dot_nt(queries[2], whole(2, 1))
+    hiddens[...] = (gate * jax.nn.sigmoid(gate) * up).astype(jnp.bfloat16)
     read_out(2)
 
     for n in range(len(pairs)):

time: 78 us -> 76.4 us (0.979)
  Pallas kernels: 75.7 us -> 74.1 us
    pallas_call x1, Pallas kernels: 75.7 us -> 74.1 us  [fused_shards(): pl.pallas_call(kernel, out_shape=jax.ShapeDtypeStruct(query.shape, low),...]
where the time goes in v3:
time: 76.4 us; the launch traced here: 76.2 us
  Pallas kernels  74.1 us (97%)
  local copies, waits for them, and re-layouts  2.06 us (3%)
    pallas_call x1, Pallas kernels, fused_shards(): pl.pallas_call(kernel, out_shape=jax.ShapeDtypeStruct(query.shape, low),...  74.1 us
    unnamed x1, local copies, waits for them, and re-layouts  2.06 us

profile of v3, /device:TPU:0, one launch (start us, length us, event | category | flops | bytes accessed | tf_op | source)
XLA Modules:
  0.0 76.2 jit_solution(6399313070502411171)
XLA Ops:
  0.0 74.1 %shard_map.82 = bf16[3,128,1024]{2,1,0:T(8,128)(2,1)} custom-call(bf16[3,128,1024]{2,1,0:T(8,128)(2,1)} %query_ref.1, bf16[3,128,1024]{2,1,0:T(8,128)(2,1)} %key_ref.1, bf16[3,128,1024]{2,1,0:T(8,128)(2,1)} %value_ref.1, f32[3,2,128]{2,1,0:T(2,128)} %bitcast.1, bf16[2,32,512]{2,1,0:T(8,128)(2,1)} %first_ref.1, bf16[2,32,512]{2,1,0:T(8,128)(2,1)} %third_ref.1, ...), custom_call_target="tpu_custom_call" | custom-call | tf_op jit(solution)/shard_map/pallas_call | solution.py:418
  74.1 2.1 %copy.10 = bf16[3,128,1024]{2,1,0:T(8,128)(2,1)} copy(bf16[3,128,1024]{2,1,0:T(8,128)(2,1)} %shard_map.82) | data formatting | bytes 1572864

commit v4 on v3

--- a/solution.py
+++ b/solution.py
@@ -198,7 +198,7 @@
     def block_of(k, m, p, q):
         return full.at[k, m, p, :, q, core]
 
-    def gather_copy(k, m, n):
+    def gather_copy(k, m, n, u=None):
         p, q = (
             (pair, lane),
             (pair, lane),
@@ -208,26 +208,30 @@
             (pair, 1 - lane),
             (1 - pair, 1 - lane),
         )[n]
-        span = block_of(k, m, p, q)
+        if u is None:
+            span, j = block_of(k, m, p, q), m
+        else:
+            owner = head if u == 0 else 1 - head
+            span, j = full.at[k, m, p, owner, q, core], 2 * m + u
         to = (beyond, beside, beside, partner, partner, partner, partner)[n]
-        return push(span, span, gather_send.at[k, m, n], gather_recv.at[k, m, n], to)
-
-    def gather_own(k, m):
+        return push(span, span, gather_send.at[k, j, n], gather_recv.at[k, j, n], to)
+
+    def gather_own(k, m, u=None):
         for n in (0, 1, 3):
-            go(gather_copy(k, m, n))
-
-    def gather_beyond(k, m):
-        gather_copy(k, m, 0).wait_recv()
-        go(gather_copy(k, m, 2))
-        go(gather_copy(k, m, 4))
-
-    def gather_beside(k, m, n):
-        gather_copy(k, m, n).wait_recv()
-        go(gather_copy(k, m, n + 4))
-
-    def gather_end(k, m):
+            go(gather_copy(k, m, n, u))
+
+    def gather_beyond(k, m, u=None):
+        gather_copy(k, m, 0, u).wait_recv()
+        go(gather_copy(k, m, 2, u))
+        go(gather_copy(k, m, 4, u))
+
+    def gather_beside(k, m, n, u=None):
+        gather_copy(k, m, n, u).wait_recv()
+        go(gather_copy(k, m, n + 4, u))
+
+    def gather_end(k, m, u=None):
         for n in range(3, 7):
-            gather_copy(k, m, n).wait_recv()
+            gather_copy(k, m, n, u).wait_recv()
 
     def core_copy(t):
         return push(
@@ -310,7 +314,8 @@
         hiddens[...] = hidden
 
     def read_out(k):
-        result[k] = dot_nt(hiddens[...], whole(k, 2)).astype(jnp.bfloat16)
+        second = whole(k, 2)
+        result[k, other_slot, :] = dot_nt(hiddens[other_slot, :], second).astype(jnp.bfloat16)
         away = push(
             result.at[k, other_slot, :],
             out_ref.at[k, :, mine],
@@ -319,6 +324,7 @@
             mate,
         )
         away.start()
+        result[k, slot, :] = dot_nt(hiddens[slot, :], second).astype(jnp.bfloat16)
         here = pltpu.make_async_copy(
             result.at[k, slot, :], out_ref.at[k, :, mine], out_local.at[k]
         )
@@ -327,16 +333,22 @@
 
     swap(0, 3)
     for m in range(3):
-        ready(m)
-        gather_own(0, m)
+        locals_[m].wait()
+        gather_own(0, m, 0)
+    for m in range(3):
+        swaps[m].wait_recv()
+        gather_own(0, m, 1)
     swap(3, 9)
-    for m in range(3):
-        gather_beyond(0, m)
-        gather_beside(0, m, 1)
-    for m in range(3):
-        gather_beside(0, m, 2)
-    for m in range(3):
-        gather_end(0, m)
+    for u in range(2):
+        for m in range(3):
+            gather_beyond(0, m, u)
+            gather_beside(0, m, 1, u)
+    for u in range(2):
+        for m in range(3):
+            gather_beside(0, m, 2, u)
+    for u in range(2):
+        for m in range(3):
+            gather_end(0, m, u)
     for n in range(3, 6):
         ready(n)
     keys_forward(0)
@@ -442,8 +454,8 @@
             dma((12,)),
             dma((12,)),
             dma((12,)),
-            dma((3, 3, 7)),
-            dma((3, 3, 7)),
+            dma((3, 6, 7)),
+            dma((3, 6, 7)),
             dma((6, 4)),
             dma((6, 4)),
             dma((3,)),

time: 76.4 us -> 77.8 us (1.018)
  Pallas kernels: 74.1 us -> 75.5 us
    pallas_call x1, Pallas kernels: 74.1 us -> 75.5 us  [fused_shards(): pl.pallas_call(kernel, out_shape=jax.ShapeDtypeStruct(query.shape, low),...]
where the time goes in v4:
time: 77.8 us; the launch traced here: 77.6 us
  Pallas kernels  75.5 us (97%)
  local copies, waits for them, and re-layouts  2.06 us (3%)
    pallas_call x1, Pallas kernels, fused_shards(): pl.pallas_call(kernel, out_shape=jax.ShapeDtypeStruct(query.shape, low),...  75.5 us
    unnamed x1, local copies, waits for them, and re-layouts  2.06 us

profile of v4, /device:TPU:0, one launch (start us, length us, event | category | flops | bytes accessed | tf_op | source)
XLA Modules:
  0.0 77.6 jit_solution(16428476626805652772)
XLA Ops:
  0.0 75.5 %shard_map.82 = bf16[3,128,1024]{2,1,0:T(8,128)(2,1)} custom-call(bf16[3,128,1024]{2,1,0:T(8,128)(2,1)} %query_ref.1, bf16[3,128,1024]{2,1,0:T(8,128)(2,1)} %key_ref.1, bf16[3,128,1024]{2,1,0:T(8,128)(2,1)} %value_ref.1, f32[3,2,128]{2,1,0:T(2,128)} %bitcast.1, bf16[2,32,512]{2,1,0:T(8,128)(2,1)} %first_ref.1, bf16[2,32,512]{2,1,0:T(8,128)(2,1)} %third_ref.1, ...), custom_call_target="tpu_custom_call" | custom-call | tf_op jit(solution)/shard_map/pallas_call | solution.py:430
  75.5 2.1 %copy.10 = bf16[3,128,1024]{2,1,0:T(8,128)(2,1)} copy(bf16[3,128,1024]{2,1,0:T(8,128)(2,1)} %shard_map.82) | data formatting | bytes 1572864

commit v5 on v3

--- a/solution.py
+++ b/solution.py
@@ -125,6 +125,8 @@
     local_sem,
     gather_send,
     gather_recv,
+    share_send,
+    share_recv,
     sum_send,
     sum_recv,
     out_send,
@@ -136,6 +138,8 @@
     lane = (index // 2) % 2
     head = (index // 4) % 2
     pair = index // 8
+    group = lax.axis_index("groups")
+    across = {"groups": 1 - group}
     partner = {"tok": index + 1 - 2 * core}
     beside = {"tok": index + 2 - 4 * lane}
     mate = {"tok": index + 4 - 8 * head}
@@ -146,9 +150,9 @@
     hidden_units = 16 * rows
 
     barrier = pltpu.get_barrier_semaphore()
-    for other in (partner, beside, mate, beyond):
+    for other in (partner, beside, mate, beyond, across):
         pl.semaphore_signal(barrier, inc=1, device_id=other, device_id_type=MESH)
-    pl.semaphore_wait(barrier, 4)
+    pl.semaphore_wait(barrier, 5)
 
     sent = []
 
@@ -211,6 +215,38 @@
         span = block_of(k, m, p, q)
         to = (beyond, beside, beside, partner, partner, partner, partner)[n]
         return push(span, span, gather_send.at[k, m, n], gather_recv.at[k, m, n], to)
+
+    share = pl.ds(pl.multiple_of(group * (width // 2), width // 2), width // 2)
+
+    def share_copy(m, n):
+        copy_from, to = (
+            ((pair, lane), beyond),
+            ((pair, lane), beside),
+            ((1 - pair, lane), beside),
+            ((1 - pair, lane), across),
+            ((pair, 1 - lane), across),
+            ((1 - pair, 1 - lane), across),
+        )[n]
+        span = full.at[0, m, copy_from[0], :, copy_from[1], core, :, share]
+        return push(span, span, share_send.at[m, n], share_recv.at[m, n], to)
+
+    def share_all():
+        for m in range(3):
+            share_copy(m, 0).wait_recv()
+            go(share_copy(m, 2))
+            go(share_copy(m, 3))
+            share_copy(m, 1).wait_recv()
+            go(share_copy(m, 4))
+        for m in range(3):
+            share_copy(m, 3).wait_recv()
+            go(gather_copy(0, m, 4))
+            share_copy(m, 2).wait_recv()
+            go(share_copy(m, 5))
+            share_copy(m, 4).wait_recv()
+            go(gather_copy(0, m, 5))
+        for m in range(3):
+            share_copy(m, 5).wait_recv()
+            go(gather_copy(0, m, 6))
 
     def gather_own(k, m):
         for n in (0, 1, 3):
@@ -328,13 +364,11 @@
     swap(0, 3)
     for m in range(3):
         ready(m)
-        gather_own(0, m)
+        go(share_copy(m, 0))
+        go(share_copy(m, 1))
+        go(gather_copy(0, m, 3))
     swap(3, 9)
-    for m in range(3):
-        gather_beyond(0, m)
-        gather_beside(0, m, 1)
-    for m in range(3):
-        gather_beside(0, m, 2)
+    share_all()
     for m in range(3):
         gather_end(0, m)
     for n in range(3, 6):
@@ -444,6 +478,8 @@
             dma((12,)),
             dma((3, 3, 7)),
             dma((3, 3, 7)),
+            dma((3, 6)),
+            dma((3, 6)),
             dma((6, 4)),
             dma((6, 4)),
             dma((3,)),
@@ -471,7 +507,7 @@
 
     def body(*arrays):
         rows = arrays[4].shape[1]
-        if rows % 16 or chips != 8 or arrays[4].shape[0] != 2:
+        if rows % 16 or chips != 8 or arrays[4].shape[0] != 2 or mesh.shape["groups"] != 2:
             return shards(*arrays)
         return fused_shards(*arrays)
 

time: 76.4 us -> 75.1 us (0.983)
  Pallas kernels: 74.1 us -> 72.9 us
    pallas_call x1, Pallas kernels: 74.1 us -> 72.9 us  [fused_shards(): pl.pallas_call(kernel, out_shape=jax.ShapeDtypeStruct(query.shape, low),...]
where the time goes in v5:
time: 75.1 us; the launch traced here: 75 us
  Pallas kernels  72.9 us (97%)
  local copies, waits for them, and re-layouts  2.06 us (3%)
    pallas_call x1, Pallas kernels, fused_shards(): pl.pallas_call(kernel, out_shape=jax.ShapeDtypeStruct(query.shape, low),...  72.9 us
    unnamed x1, local copies, waits for them, and re-layouts  2.06 us

profile of v5, /device:TPU:0, one launch (start us, length us, event | category | flops | bytes accessed | tf_op | source)
XLA Modules:
  0.0 75.0 jit_solution(15360866596358594528)
XLA Ops:
  0.0 72.9 %shard_map.82 = bf16[3,128,1024]{2,1,0:T(8,128)(2,1)} custom-call(bf16[3,128,1024]{2,1,0:T(8,128)(2,1)} %query_ref.1, bf16[3,128,1024]{2,1,0:T(8,128)(2,1)} %key_ref.1, bf16[3,128,1024]{2,1,0:T(8,128)(2,1)} %value_ref.1, f32[3,2,128]{2,1,0:T(2,128)} %bitcast.1, bf16[2,32,512]{2,1,0:T(8,128)(2,1)} %first_ref.1, bf16[2,32,512]{2,1,0:T(8,128)(2,1)} %third_ref.1, ...), custom_call_target="tpu_custom_call" | custom-call | tf_op jit(solution)/shard_map/pallas_call | solution.py:452
  72.9 2.1 %copy.10 = bf16[3,128,1024]{2,1,0:T(8,128)(2,1)} copy(bf16[3,128,1024]{2,1,0:T(8,128)(2,1)} %shard_map.82) | data formatting | bytes 1572864
